TPU v7x, 512 devices: a whole 4x8x8 slice. The times are simulated.
512 devices in a mesh: img: 8 (over y_lo, core), cin: 8 (over x, y_hi), cout: 8 (over z).
Axes of the slice: x: 4, y: 8 (y_hi: 2, y_lo: 4; y = y_hi * 4 + y_lo), z: 8, core: 2. Of those that a mesh axis runs over, the one named last changes fastest.
Arguments:
- maps: bfloat16 [2, 8, 14, 14, 1024], P(None, 'img'), may hold values from -6 to 6
- w_first: bfloat16 [3, 3, 1024, 1024], P(None, None, 'cin', 'cout'), may hold values from -0.09375 to 0.09375
- w_reduce: bfloat16 [3, 3, 1024, 8192], P(None, None, 'img', ('cin', 'cout')), may hold values from -0.09375 to 0.09375
- w_wide: bfloat16 [3, 3, 8192, 8192], P(None, None, 'cin', ('img', 'cout')), may hold values from -0.03125 to 0.03125
Outputs:
- wide_out: bfloat16 [2, 8, 7, 7, 8192], P(None, 'cin', None, None, ('img', 'cout'))
All inputs are finite; a program needn't handle non-finite values.
Results may differ from a plain program's by a relative error of at most 0.014.
Values may be sent and summed in bfloat16 or wider, within the bound.
No kernel may reach another device: no remote copies, remote signals or barrier semaphores. Data moves between devices by JAX's collectives and lax.ppermute only.
A program may use at most 64 MiB of HBM per device.

v0:
```python
import jax
import jax.numpy as jnp
from jax import lax
from jax.sharding import PartitionSpec as P


def conv_block(padded, weight_flat, size, step):
    channels = padded.shape[3]
    windows = []
    for row_tap in range(3):
        for col_tap in range(3):
            windows.append(
                padded[
                    :,
                    row_tap : row_tap + step * (size - 1) + 1 : step,
                    col_tap : col_tap + step * (size - 1) + 1 : step,
                    :,
                ]
            )
    table = jnp.concatenate(windows, axis=3).reshape(-1, 9 * channels)
    total = jnp.dot(table, weight_flat, preferred_element_type=jnp.float32)
    return total.reshape(padded.shape[0], size, size, weight_flat.shape[1])


def conv_taps(padded, weight, size, step):
    count = padded.shape[0]
    channels = padded.shape[3]
    weight_flat = weight.reshape(9 * channels, weight.shape[3])
    group = 1
    for trial in range(1, 9):
        if count % trial == 0:
            group = trial
    blocks = padded.reshape(count // group, group, padded.shape[1], padded.shape[2], channels)
    results = lax.map(lambda block: conv_block(block, weight_flat, size, step), blocks)
    return results.reshape(count, size, size, weight.shape[3])


def pad_map(values):
    return jnp.pad(values, ((0, 0), (1, 1), (1, 1), (0, 0)))


def local(maps, w_first, w_reduce, w_wide):
    batches = maps.shape[0]
    side = maps.shape[2]
    half = side // 2
    in_block = w_first.shape[2]
    out_block = w_first.shape[3]
    flat = maps.reshape(-1, side, side, maps.shape[4])
    in_part = lax.dynamic_slice_in_dim(flat, lax.axis_index("cin") * in_block, in_block, 3)
    first_terms = conv_taps(pad_map(jnp.maximum(in_part, 0)), w_first, side, 1)
    first_terms = first_terms.reshape(batches, maps.shape[1], side, side, out_block)
    summed = lax.psum(first_terms, "cin")
    own_part = lax.dynamic_slice_in_dim(maps, lax.axis_index("cout") * out_block, out_block, 4)
    segment_maps = (own_part.astype(jnp.float32) + summed).astype(jnp.bfloat16)
    whole = lax.all_gather(segment_maps, "cout", axis=4, tiled=True)
    by_channel = lax.all_to_all(whole, "img", split_axis=4, concat_axis=1, tiled=True)
    images = by_channel.shape[1]
    rect_segment = jnp.maximum(by_channel, 0).reshape(-1, side, side, by_channel.shape[4])
    reduced = conv_taps(pad_map(rect_segment), w_reduce, half, 2).reshape(
        batches, images, half, half, w_reduce.shape[3]
    )
    out_width = w_wide.shape[3]
    summed_wide = lax.psum(reduced, "img")
    narrow = jnp.maximum(summed_wide, 0.0).astype(jnp.bfloat16)
    gathered = lax.all_gather(narrow, "cout", axis=4, tiled=True)
    flat_all = gathered.reshape(-1, half, half, gathered.shape[4])
    partial_value = conv_taps(pad_map(flat_all), w_wide, half, 1)
    partial_value = partial_value.reshape(batches, images, half, half, out_width)
    result = lax.psum_scatter(
        partial_value.astype(jnp.bfloat16), "cin", scatter_dimension=1, tiled=True
    )
    return result


def solution(mesh):
    in_specs = (
        P(None, "img", None, None, None),
        P(None, None, "cin", "cout"),
        P(None, None, "img", ("cin", "cout")),
        P(None, None, "cin", ("img", "cout")),
    )
    out_specs = P(None, "cin", None, None, ("img", "cout"))
    return jax.shard_map(local, mesh=mesh, in_specs=in_specs, out_specs=out_specs, check_vma=False)
```

profile of v0, /device:TPU:64, one launch (start us, length us, event | category | flops | bytes accessed | tf_op | source)
XLA Modules:
  0.0 461.7 jit_solution(14591765025077755233)
XLA Ops:
  6.5 1.1 constant_dynamic-slice_fusion.2
  8.2 1.1 convolution_bitcast_fusion.1
  9.3 116.6 %all-reduce.8.cloned.1.call-done = f32[2,1,14,14,128]{4,3,2,0,1:T(8,128)} async-done(((f32[2,1,14,14,128]{4,3,2,0,1:T(8,128)}), f32[2,1,14,14,128]{4,3,2,0,1:T(8,128)}) %all-reduce.8.cloned.1.call-update) | async-done | bytes 200720 | tf_op jit(solution)/shard_map/psum | solution.py:52
  126.0 1.0 add_convert_fusion
  126.9 26.5 %all_gather.6 = bf16[2,1,14,14,1024]{4,3,2,0,1:T(8,128)(2,1)S(1)} all-gather(bf16[2,1,14,14,128]{4,3,2,0,1:T(8,128)(2,1)S(1)} %add_convert_fusion), channel_id=1, replica_groups=mesh['img'=8,'cin'=8,'cout'=8] {'cout'}, dimensions={4}, use_global_device_ids=true | all-gather | bytes 903168 | tf_op jit(solution)/shard_map/all_gather | solution.py:55
  153.5 12.4 %copy.42 = bf16[2,1,14,14,1024]{3,0,2,1,4:T(2,128)(2,1)} copy(bf16[2,1,14,14,1024]{4,3,2,0,1:T(8,128)(2,1)S(1)} %all_gather.6) | data formatting | bytes 1605632 | tf_op jit(solution)/shard_map/all_gather | solution.py:55
  165.8 12.8 %reshape.68 = bf16[8,2,25088]{2,1,0:T(2,128)(2,1)} reshape(bf16[1024,1,14,2,14]{4,3,2,1,0:T(2,128)(2,1)} %bitcast.84) | data formatting | bytes 1605632
  178.7 3.5 all-to-all-start
  182.3 21.2 %all-to-all-done = bf16[8,2,25088]{2,1,0:T(2,128)(2,1)S(1)} async-done(((bf16[8,2,25088]{2,1,0:T(2,128)(2,1)}), bf16[8,2,25088]{2,1,0:T(2,128)(2,1)S(1)}, u32[]{:S(2)}, u32[]{:S(2)}) %all-to-all-start) | async-done | bytes 802848 | tf_op jit(solution)/shard_map/all_to_all | solution.py:56
  203.4 19.8 %reshape.69 = bf16[1024,1,14,2,14]{4,3,2,1,0:T(2,128)(2,1)} reshape(bf16[8,2,25088]{2,1,0:T(2,128)(2,1)S(1)} %all-to-all-done) | data formatting | bytes 1605632
  223.2 17.3 %copy.43 = bf16[2,1,14,14,1024]{4,0,3,2,1:T(2,128)(2,1)S(1)} copy(bf16[2,1,14,14,1024]{3,0,2,1,4:T(2,128)(2,1)} %bitcast.85) | data formatting | bytes 1605632 | tf_op jit(solution)/shard_map/all_to_all | solution.py:56
  240.5 0.7 broadcast_maximum_fusion
  241.2 0.5 max.33
  241.7 1.2 pad_bitcast_fusion.1
  242.9 4.0 while.26
  242.9 1.2 dynamic-slice_bitcast_fusion.6
  245.0 1.1 dynamic-slice_bitcast_fusion.6
  246.9 31.9 %all-reduce.11 = bf16[2,8,7,7,128]{4,1,0,3,2:T(8,128)(2,1)S(1)} all-reduce(f32[2,8,7,7,128]{4,1,0,3,2:T(8,128)S(1)} %get-tuple-element.61), channel_id=1, replica_groups=mesh['img'=8,'cin'=8,'cout'=8] {'img'}, use_global_device_ids=true, to_apply=%region_3.4 | all-reduce | flops 100352 | bytes 602112 | tf_op jit(solution)/shard_map/psum | solution.py:63
  278.8 0.7 maximum_convert_fusion
  279.6 41.6 %all-gather.2.cloned.1.call-done = bf16[2,8,7,7,1024]{4,1,0,3,2:T(8,128)(2,1)} async-done(((bf16[2,8,7,7,128]{4,1,0,3,2:T(8,128)(2,1)}), bf16[2,8,7,7,1024]{4,1,0,3,2:T(8,128)(2,1)}) %all-gather.2.cloned.1.call-update) | async-done | bytes 1605648 | tf_op jit(solution)/shard_map/all_gather | solution.py:65
  321.2 3.3 pad_bitcast_fusion
  324.5 17.2 %while.27 = (s32[]{:T(128)}, bf16[2,8,7,7,128]{4,0,3,2,1:T(2,128)(2,1)S(1)}, bf16[2,8,9,9,1024]{4,1,0,3,2:T(8,128)(2,1)}, bf16[9216,128]{1,0:T(8,128)(2,1)S(1)}) while((s32[]{:T(128)}, bf16[2,8,7,7,128]{4,0,3,2,1:T(2,128)(2,1)S(1)}, bf16[2,8,9,9,1024]{4,1,0,3,2:T(8,128)(2,1)}, bf16[9216,128]{1,0:T(8,128)(2,1)S(1)}) %tuple.60), condition=%wide.region_5.6_spmd.clone, body=%wide.region_4.5_spmd.sunk.clone | while | flops 924844032 | bytes 27191356 | solution.py:34
  324.5 1.4 dynamic-slice_bitcast_fusion.7
  326.5 2.0 fusion.29
  328.7 4.4 dynamic_update_slice.16
  333.1 1.4 dynamic-slice_bitcast_fusion.7
  335.1 2.0 fusion.29
  337.3 4.4 dynamic_update_slice.16
  341.8 0.7 copy-done.3
  342.5 1.3 dynamic-slice.2
  343.7 109.5 %all-reduce.10.cloned.1.call-done = bf16[2,8,7,7,128]{4,0,3,2,1:T(2,128)(2,1)} async-done(((bf16[2,8,7,7,128]{4,0,3,2,1:T(2,128)(2,1)}), bf16[2,8,7,7,128]{4,0,3,2,1:T(2,128)(2,1)}) %all-reduce.10.cloned.1.call-update) | async-done | bytes 200720
  453.3 1.9 constant_dynamic-slice_fusion
  (65 shorter events, 3.4 us)
Async XLA Ops:
  6.5 1.6 copy-start
  6.5 119.4 %all-reduce.8.cloned.1.call-start = ((), (), s32[]{:S(2)}) async-start(), calls=%async_computation.1 | async-start | bytes 458752 | tf_op jit(solution)/shard_map/psum | solution.py:52
  178.7 24.8 %all-to-all-start = ((bf16[8,2,25088]{2,1,0:T(2,128)(2,1)}), bf16[8,2,25088]{2,1,0:T(2,128)(2,1)S(1)}, u32[]{:S(2)}, u32[]{:S(2)}) async-start(bf16[8,2,25088]{2,1,0:T(2,128)(2,1)} %reshape.68), calls=%async_computation | async-start | bytes 1605632 | tf_op jit(solution)/shard_map/all_to_all | solution.py:56
  182.2 139.0 %all-gather.2.cloned.1.call-start = ((), (), s32[]{:S(2)}) async-start(), calls=%async_computation.2 | async-start | bytes 1806336 | tf_op jit(solution)/shard_map/all_gather | solution.py:65
  223.2 19.7 %copy-start.2 = (bf16[3,3,128,128]{3,2,1,0:T(8,128)(2,1)S(1)}, bf16[3,3,128,128]{3,2,1,0:T(8,128)(2,1)}, u32[]{:S(2)}) copy-start(bf16[3,3,128,128]{3,2,1,0:T(8,128)(2,1)} %param.10) | copy-start | bytes 884740
  242.9 81.6 %copy-start.1 = (bf16[3,3,1024,128]{3,2,1,0:T(8,128)(2,1)S(1)}, bf16[3,3,1024,128]{3,2,1,0:T(8,128)(2,1)}, u32[]{:S(2)}) copy-start(bf16[3,3,1024,128]{3,2,1,0:T(8,128)(2,1)} %param.11) | copy-start | bytes 7077892
  279.5 173.7 %all-reduce.10.cloned.1.call-start = ((), (), s32[]{:S(2)}) async-start(), calls=%async_computation.3 | async-start | bytes 401408
  341.8 0.7 copy-start.3
Sparse Core Ops, SparseCore 0:
  10.3 115.6 all-reduce.7
  279.6 41.5 all-gather.1
  342.6 110.6 all-reduce.9
where the time goes:
time: 463 us; the launch traced here: 462 us
  waiting for transfers between devices  289 us (62%)
  local copies, waits for them, and re-layouts  88.5 us (19%)
  blocking collectives  58.4 us (13%)
  between operations  13.3 us (3%)
  matrix products  6.06 us (1%)
    psum x1, waiting for transfers between devices, local(): summed = lax.psum(first_terms, 'cin')  117 us
    unnamed x4, waiting for transfers between devices  110 us
    all_gather x1, waiting for transfers between devices, local(): gathered = lax.all_gather(narrow, 'cout', axis=4, tiled=True)  41.6 us
    unnamed x19, local copies, waits for them, and re-layouts  36.8 us
    psum x1, blocking collectives, local(): summed_wide = lax.psum(reduced, 'img')  31.9 us
    all_gather x1, blocking collectives, local(): whole = lax.all_gather(segment_maps, 'cout', axis=4, tiled=True)  26.5 us
    all_to_all x1, waiting for transfers between devices, local(): lax.all_to_all(whole, 'img', split_axis=4, concat_axis=1, tiled=True)  21.2 us
    all_to_all x1, local copies, waits for them, and re-layouts, local(): lax.all_to_all(whole, 'img', split_axis=4, concat_axis=1, tiled=True)  17.3 us
  transfers between devices with their start and end apart: 4, of which 4 were waited for; matrix products, arithmetic and copies ran while one was open for 0% of the time, Pallas kernels for 0%

commit v1 on v0

--- a/solution.py
+++ b/solution.py
@@ -2,6 +2,14 @@
 import jax.numpy as jnp
 from jax import lax
 from jax.sharding import PartitionSpec as P
+
+
+def number_view(z, where_dim):
+    upper = jnp.concatenate(
+        jax.lax.all_to_all(jnp.stack([z for _ in range(jax.lax.axis_size("cout"))]), "cout", 0, 0),
+        where_dim,
+    )
+    return upper
 
 
 def conv_block(padded, weight_flat, size, step):
@@ -52,7 +60,7 @@
     summed = lax.psum(first_terms, "cin")
     own_part = lax.dynamic_slice_in_dim(maps, lax.axis_index("cout") * out_block, out_block, 4)
     segment_maps = (own_part.astype(jnp.float32) + summed).astype(jnp.bfloat16)
-    whole = lax.all_gather(segment_maps, "cout", axis=4, tiled=True)
+    whole = number_view(segment_maps, 4)
     by_channel = lax.all_to_all(whole, "img", split_axis=4, concat_axis=1, tiled=True)
     images = by_channel.shape[1]
     rect_segment = jnp.maximum(by_channel, 0).reshape(-1, side, side, by_channel.shape[4])

time: 463 us -> 458 us (0.989)
    all_gather x1 -> x0, blocking collectives: 26.5 us -> none  [local(): whole = lax.all_gather(segment_maps, 'cout', axis=4, tiled=True)]
    all_to_all x0 -> x1, blocking collectives: none -> 24.3 us  [number_view(): jax.lax.all_to_all(jnp.stack([z for _ in range(jax.lax.axis_size('cout'))...]
    all_gather x1 -> x0, local copies, waits for them, and re-layouts: 12.4 us -> none  [local(): whole = lax.all_gather(segment_maps, 'cout', axis=4, tiled=True)]
    reshape x0 -> x1, local copies, waits for them, and re-layouts: none -> 12.3 us  [number_view(): jnp.concatenate(jax.lax.all_to_all(jnp.stack([z for _ in range(jax.lax.ax...]
where the time goes in v1:
time: 458 us; the launch traced here: 457 us
  waiting for transfers between devices  286 us (62%)
  local copies, waits for them, and re-layouts  88.9 us (19%)
  blocking collectives  56.2 us (12%)
  between operations  13.3 us (3%)
  matrix products  6.06 us (1%)
    psum x1, waiting for transfers between devices, local(): summed = lax.psum(first_terms, 'cin')  117 us
    unnamed x4, waiting for transfers between devices  110 us
    all_gather x1, waiting for transfers between devices, local(): gathered = lax.all_gather(narrow, 'cout', axis=4, tiled=True)  38.5 us
    unnamed x19, local copies, waits for them, and re-layouts  36.8 us
    psum x1, blocking collectives, local(): summed_wide = lax.psum(reduced, 'img')  31.9 us
    all_to_all x1, blocking collectives, number_view(): jax.lax.all_to_all(jnp.stack([z for _ in range(jax.lax.axis_size('cout'))...  24.3 us
    all_to_all x1, waiting for transfers between devices, local(): lax.all_to_all(whole, 'img', split_axis=4, concat_axis=1, tiled=True)  21.2 us
    all_to_all x1, local copies, waits for them, and re-layouts, local(): lax.all_to_all(whole, 'img', split_axis=4, concat_axis=1, tiled=True)  17.3 us
  transfers between devices with their start and end apart: 4, of which 4 were waited for; matrix products, arithmetic and copies ran while one was open for 0% of the time, Pallas kernels for 0%

profile of v1, /device:TPU:64, one launch (start us, length us, event | category | flops | bytes accessed | tf_op | source)
XLA Modules:
  0.0 456.9 jit_solution(2806415963040960365)
XLA Ops:
  6.5 1.1 constant_dynamic-slice_fusion.2
  8.2 1.1 convolution_bitcast_fusion.1
  9.3 116.6 %all-reduce.8.cloned.1.call-done = f32[2,1,14,14,128]{4,3,2,0,1:T(8,128)} async-done(((f32[2,1,14,14,128]{4,3,2,0,1:T(8,128)}), f32[2,1,14,14,128]{4,3,2,0,1:T(8,128)}) %all-reduce.8.cloned.1.call-update) | async-done | bytes 200720 | tf_op jit(solution)/shard_map/psum | solution.py:60
  126.0 1.0 fusion.7
  127.5 24.3 %all_to_all.14 = bf16[8,2,1,14,14,128]{5,1,4,3,2,0:T(2,128)(2,1)S(1)} all-to-all(bf16[8,2,1,14,14,128]{5,1,4,3,2,0:T(2,128)(2,1)S(1)} %stack.2), channel_id=1, replica_groups=mesh['img'=8,'cin'=8,'cout'=8] {'cout'}, dimensions={0} | all-to-all | bytes 1605632 | tf_op jit(solution)/shard_map/all_to_all | solution.py:9
  151.7 12.3 %copy.60 = bf16[2,1,14,14,8,128]{3,0,2,5,4,1:T(2,128)(2,1)} copy(bf16[2,1,14,14,8,128]{5,0,3,2,1,4:T(2,128)(2,1)S(1)} %bitcast.92) | data formatting | bytes 1605632 | tf_op jit(solution)/shard_map/reshape | solution.py:8
  164.0 12.8 %reshape.79 = bf16[8,2,25088]{2,1,0:T(2,128)(2,1)} reshape(bf16[1024,1,14,2,14]{4,3,2,1,0:T(2,128)(2,1)} %bitcast.88) | data formatting | bytes 1605632
  176.9 3.5 all-to-all-start.1
  180.5 21.2 %all-to-all-done.1 = bf16[8,2,25088]{2,1,0:T(2,128)(2,1)S(1)} async-done(((bf16[8,2,25088]{2,1,0:T(2,128)(2,1)}), bf16[8,2,25088]{2,1,0:T(2,128)(2,1)S(1)}, u32[]{:S(2)}, u32[]{:S(2)}) %all-to-all-start.1) | async-done | bytes 802848 | tf_op jit(solution)/shard_map/all_to_all | solution.py:64
  201.6 19.8 %reshape.80 = bf16[1024,1,14,2,14]{4,3,2,1,0:T(2,128)(2,1)} reshape(bf16[8,2,25088]{2,1,0:T(2,128)(2,1)S(1)} %all-to-all-done.1) | data formatting | bytes 1605632
  221.4 17.3 %copy.49 = bf16[2,1,14,14,1024]{4,0,3,2,1:T(2,128)(2,1)S(1)} copy(bf16[2,1,14,14,1024]{3,0,2,1,4:T(2,128)(2,1)} %bitcast.89) | data formatting | bytes 1605632 | tf_op jit(solution)/shard_map/all_to_all | solution.py:64
  238.7 0.7 broadcast_maximum_fusion
  239.4 0.5 max.33
  239.9 1.2 pad_bitcast_fusion.1
  241.1 4.0 while.26
  241.1 1.2 dynamic-slice_bitcast_fusion.6
  243.2 1.1 dynamic-slice_bitcast_fusion.6
  245.1 31.9 %all-reduce.11 = bf16[2,8,7,7,128]{4,1,0,3,2:T(8,128)(2,1)S(1)} all-reduce(f32[2,8,7,7,128]{4,1,0,3,2:T(8,128)S(1)} %get-tuple-element.61), channel_id=1, replica_groups=mesh['img'=8,'cin'=8,'cout'=8] {'img'}, use_global_device_ids=true, to_apply=%region_3.4 | all-reduce | flops 100352 | bytes 602112 | tf_op jit(solution)/shard_map/psum | solution.py:71
  277.0 0.7 maximum_convert_fusion
  278.0 38.5 %all-gather.2.cloned.1.call-done = bf16[2,8,7,7,1024]{4,1,0,3,2:T(8,128)(2,1)} async-done(((bf16[2,8,7,7,128]{4,1,0,3,2:T(8,128)(2,1)}), bf16[2,8,7,7,1024]{4,1,0,3,2:T(8,128)(2,1)}) %all-gather.2.cloned.1.call-update) | async-done | bytes 1605648 | tf_op jit(solution)/shard_map/all_gather | solution.py:73
  316.5 3.3 pad_bitcast_fusion
  319.8 17.2 %while.27 = (s32[]{:T(128)}, bf16[2,8,7,7,128]{4,0,3,2,1:T(2,128)(2,1)S(1)}, bf16[2,8,9,9,1024]{4,1,0,3,2:T(8,128)(2,1)}, bf16[9216,128]{1,0:T(8,128)(2,1)S(1)}) while((s32[]{:T(128)}, bf16[2,8,7,7,128]{4,0,3,2,1:T(2,128)(2,1)S(1)}, bf16[2,8,9,9,1024]{4,1,0,3,2:T(8,128)(2,1)}, bf16[9216,128]{1,0:T(8,128)(2,1)S(1)}) %tuple.60), condition=%wide.region_5.6_spmd.clone, body=%wide.region_4.5_spmd.sunk.clone | while | flops 924844032 | bytes 27191356 | solution.py:42
  319.8 1.4 dynamic-slice_bitcast_fusion.7
  321.8 2.0 fusion.30
  324.0 4.4 dynamic_update_slice.16
  328.4 1.4 dynamic-slice_bitcast_fusion.7
  330.4 2.0 fusion.30
  332.6 4.4 dynamic_update_slice.16
  337.0 0.7 copy-done.3
  337.7 1.3 dynamic-slice.2
  339.0 109.5 %all-reduce.10.cloned.1.call-done = bf16[2,8,7,7,128]{4,0,3,2,1:T(2,128)(2,1)} async-done(((bf16[2,8,7,7,128]{4,0,3,2,1:T(2,128)(2,1)}), bf16[2,8,7,7,128]{4,0,3,2,1:T(2,128)(2,1)}) %all-reduce.10.cloned.1.call-update) | async-done | bytes 200720
  448.5 1.9 constant_dynamic-slice_fusion
  (67 shorter events, 4.1 us)
Async XLA Ops:
  6.5 1.6 copy-start
  6.5 119.4 %all-reduce.8.cloned.1.call-start = ((), (), s32[]{:S(2)}) async-start(), calls=%async_computation.2 | async-start | bytes 458752 | tf_op jit(solution)/shard_map/psum | solution.py:60
  176.9 24.8 %all-to-all-start.1 = ((bf16[8,2,25088]{2,1,0:T(2,128)(2,1)}), bf16[8,2,25088]{2,1,0:T(2,128)(2,1)S(1)}, u32[]{:S(2)}, u32[]{:S(2)}) async-start(bf16[8,2,25088]{2,1,0:T(2,128)(2,1)} %reshape.79), calls=%async_computation.1 | async-start | bytes 1605632 | tf_op jit(solution)/shard_map/all_to_all | solution.py:64
  180.4 136.1 %all-gather.2.cloned.1.call-start = ((), (), s32[]{:S(2)}) async-start(), calls=%async_computation.3 | async-start | bytes 1806336 | tf_op jit(solution)/shard_map/all_gather | solution.py:73
  221.4 19.7 %copy-start.2 = (bf16[3,3,128,128]{3,2,1,0:T(8,128)(2,1)S(1)}, bf16[3,3,128,128]{3,2,1,0:T(8,128)(2,1)}, u32[]{:S(2)}) copy-start(bf16[3,3,128,128]{3,2,1,0:T(8,128)(2,1)} %param.10) | copy-start | bytes 884740
  241.1 78.7 %copy-start.1 = (bf16[3,3,1024,128]{3,2,1,0:T(8,128)(2,1)S(1)}, bf16[3,3,1024,128]{3,2,1,0:T(8,128)(2,1)}, u32[]{:S(2)}) copy-start(bf16[3,3,1024,128]{3,2,1,0:T(8,128)(2,1)} %param.11) | copy-start | bytes 7077892
  277.7 170.7 %all-reduce.10.cloned.1.call-start = ((), (), s32[]{:S(2)}) async-start(), calls=%async_computation.4 | async-start | bytes 401408
  337.0 0.7 copy-start.3
Sparse Core Ops, SparseCore 0:
  10.3 115.6 all-reduce.7
  277.9 38.5 all-gather.1
  337.8 110.6 all-reduce.9
